TPU v7x, 32 devices: a whole 2x2x4 slice. The times are simulated.
32 devices in a mesh: fsdp: 8 (over y, x, core), win: 4 (over z).
Axes of the slice: x: 2, y: 2, z: 4, core: 2. Of those that a mesh axis runs over, the one named last changes fastest.
Arguments:
- tokens: bfloat16 [16384, 2048], P(('fsdp', 'win')), may hold values from -16 to 16
- block_map: int32 [8, 4], P('fsdp'), may hold values from 0 to 3, each once within a row
- shift: int32 [8], P('fsdp'), may hold values from 1 to 2047
- ln_gain: float32 [2048], replicated, may hold values from 0.5 to 1.5
- w_query: bfloat16 [2048, 1024], P('fsdp'), may hold values from -1 to 1
- w_key: bfloat16 [2048, 1024], P('fsdp'), may hold values from -1 to 1
- w_value: bfloat16 [2048, 1024], P('fsdp'), may hold values from -0.125 to 0.125
- w_out: bfloat16 [1024, 2048], P('fsdp'), may hold values from -0.1875 to 0.1875
- logit_scale: float32 [16], replicated, may hold values from 1 to 300
Outputs:
- mixed: bfloat16 [16384, 2048], P(('fsdp', 'win'))
All inputs are finite; a program needn't handle non-finite values.
Results may differ from a plain program's by a relative error of at most 0.008.
Values may be sent and summed in bfloat16 or wider, within the bound.
A program may use at most 128 MiB of HBM per device.

v0:
```python
import jax
import jax.numpy as jnp
from jax import lax
from jax.sharding import PartitionSpec as P


def layer_norm(resid, gain):
    center = jnp.mean(resid, axis=-1, keepdims=True)
    centred = resid - center
    spread = jnp.mean(centred * centred, axis=-1, keepdims=True)
    return (centred * lax.rsqrt(spread + 1e-05) * gain).astype(jnp.bfloat16)


def unit_heads(values, head_count):
    split = values.reshape(values.shape[0], head_count, -1)
    scale = lax.rsqrt(jnp.sum(split * split, axis=-1, keepdims=True) + 1e-06)
    return (split * scale).astype(jnp.bfloat16)


def block_length():
    return 512


def per_device(tokens, block_map, shift, ln_gain, w_query, w_key, w_value, w_out, logit_scale):
    tok_rows = tokens.shape[0]
    head_count = logit_scale.shape[0]
    inner = w_query.shape[1]
    head_size = inner // head_count
    groups = lax.axis_size("win")
    member = lax.axis_index("win")
    block_row = block_map[0]
    offset = shift[0]
    resid = tokens.astype(jnp.float32)
    normed = layer_norm(resid, ln_gain)
    group_ids = jnp.arange(groups, dtype=jnp.int32)

    def region_of(index):
        owner = index // tok_rows
        picked = owner[:, None] == group_ids[None, :]
        block = jnp.sum(jnp.where(picked, block_row[None, :], 0), axis=1)
        return block * tok_rows + index % tok_rows >= offset

    pieces = (
        lax.all_gather(w_query, "fsdp", axis=0, tiled=True),
        lax.all_gather(w_key, "fsdp", axis=0, tiled=True),
        lax.all_gather(w_value, "fsdp", axis=0, tiled=True),
    )
    columns = normed
    query, key_full, value = tuple(
        (jnp.dot(columns, piece, preferred_element_type=jnp.float32) for piece in pieces)
    )
    q_unit = unit_heads(query, head_count)
    k_flat = unit_heads(key_full, head_count).reshape(tok_rows, inner)
    value_half = value.astype(jnp.bfloat16)
    own_region = region_of(member * tok_rows + jnp.arange(tok_rows, dtype=jnp.int32))
    start_state = (
        jnp.full((head_count, tok_rows), -1e30, jnp.float32),
        jnp.zeros((head_count, tok_rows), jnp.float32),
        jnp.zeros((tok_rows, head_count, head_size), jnp.float32),
    )

    def attend_block(carry, packed):
        best, total, accum = carry
        keys, values, regions = packed
        allowed = (own_region[:, None] == regions[None, :])[None]
        score = (
            jnp.einsum("ihd,jhd->hij", q_unit, keys, preferred_element_type=jnp.float32)
            * logit_scale[:, None, None]
        )
        score = jnp.where(allowed, score, -1e30)
        new_best = jnp.maximum(best, jnp.max(score, axis=-1))
        weight = jnp.where(allowed, jnp.exp(score - new_best[:, :, None]), 0.0)
        fade = jnp.exp(best - new_best)
        total = total * fade + jnp.sum(weight, axis=-1)
        accum = accum * fade.T[:, :, None] + jnp.einsum(
            "hij,jhd->ihd", weight.astype(jnp.bfloat16), values, preferred_element_type=jnp.float32
        )
        return ((new_best, total, accum), None)

    carry = start_state
    pieces = (
        lax.all_gather(k_flat, "win", axis=0, tiled=True),
        lax.all_gather(value_half, "win", axis=0, tiled=True),
    )
    count = pieces[0].shape[0]
    blk = block_length()
    nblk = count // blk
    keys = pieces[0].reshape(nblk, blk, head_count, head_size)
    values = pieces[1].reshape(nblk, blk, head_count, head_size)
    regions = region_of(jnp.arange(count, dtype=jnp.int32)).reshape(nblk, blk)
    carry, unused = lax.scan(attend_block, carry, (keys, values, regions))
    best, total, accum = carry
    attended = (accum / total.T[:, :, None]).reshape(tok_rows, inner).astype(jnp.bfloat16)
    columns = attended
    output_sum = jnp.dot(
        columns,
        lax.all_gather(w_out, "fsdp", axis=0, tiled=True),
        preferred_element_type=jnp.float32,
    )
    return (resid + output_sum).astype(jnp.bfloat16)


def solution(mesh):
    return jax.shard_map(
        per_device,
        mesh=mesh,
        in_specs=(
            P(("fsdp", "win"), None),
            P("fsdp", None),
            P("fsdp"),
            P(),
            P("fsdp", None),
            P("fsdp", None),
            P("fsdp", None),
            P("fsdp", None),
            P(),
        ),
        out_specs=P(("fsdp", "win"), None),
        check_vma=False,
    )
```

profile of v0, /device:TPU:0, one launch (start us, length us, event | category | flops | bytes accessed | tf_op | source)
XLA Modules:
  0.0 430.1 jit_solution(9494824374934924594)
XLA Ops:
  6.5 0.0 all-gather.7.cloned.1.call-start
  6.5 0.7 all-gather.7.cloned.1.call-update
  7.3 0.0 all-gather.13.cloned.1.call-start
  7.3 0.7 all-gather.13.cloned.1.call-update
  8.0 0.0 all-gather.11.cloned.1.call-start
  8.1 0.7 all-gather.11.cloned.1.call-update
  8.7 0.0 all-gather.9.cloned.1.call-start
  8.8 1.9 convert_reduce_fusion
  10.7 0.0 copy-done.1
  10.8 0.7 fusion.21
  11.4 37.3 %all-gather.7.cloned.1.call-done = bf16[2048,1024]{1,0:T(8,128)(2,1)} async-done(((bf16[256,1024]{1,0:T(8,128)(2,1)}), bf16[2048,1024]{1,0:T(8,128)(2,1)}) %all-gather.7.cloned.1.call-update) | async-done | bytes 4194320 | tf_op jit(solution)/shard_map/all_gather | solution.py:45
  48.7 0.0 copy-done.4
  48.7 6.6 %fusion.41 = (f32[512,1024]{1,0:T(8,128)}, f32[512,1024]{1,0:T(8,128)}) fusion(bf16[2048,1024]{1,0:T(8,128)(2,1)} %all-gather.7.cloned.1.call-done, bf16[512,2048]{1,0:T(8,128)(2,1)S(1)} %copy-done.1, f32[2048]{0:T(1024)S(1)} %copy-done.4, f32[512]{0:T(512)S(1)} %add_rsqrt_fusion.2, f32[512]{0:T(512)S(1)} %broadcast_multiply_fusion.1), kind=kOutput, calls=%fused_computation.76 | convolution fusion | flops 2153250816 | bytes 10498048 | tf_op jit(solution)/shard_map/dot_general | solution.py:50
  55.3 2.9 copy.24
  58.2 2.0 bitcast_reduce_fusion
  60.3 1.6 mul.95
  61.9 2.9 copy.25
  64.8 3.5 multiply_convert_fusion.1
  68.3 0.0 all-gather.9.cloned.1.call-update
  68.3 0.0 copy-start.3
  68.4 0.0 all-gather.15.cloned.1.call-start
  68.4 18.9 %all-gather.13.cloned.1.call-done = bf16[2048,1024]{1,0:T(8,128)(2,1)} async-done(((bf16[256,1024]{1,0:T(8,128)(2,1)}), bf16[2048,1024]{1,0:T(8,128)(2,1)}) %all-gather.13.cloned.1.call-update) | async-done | bytes 4194320 | tf_op jit(solution)/shard_map/all_gather | solution.py:46
  87.3 5.6 %convolution_convert_fusion = bf16[512,1024]{1,0:T(8,128)(2,1)} fusion(bf16[2048,1024]{1,0:T(8,128)(2,1)} %all-gather.13.cloned.1.call-done, bf16[512,2048]{1,0:T(8,128)(2,1)S(1)} %copy-done.1, f32[2048]{0:T(1024)S(1)} %copy-done.4, f32[512]{0:T(512)S(1)} %add_rsqrt_fusion.2, f32[512]{0:T(512)S(1)} %broadcast_multiply_fusion.1), kind=kOutput, calls=%fused_computation.39 | convolution fusion | flops 2153250816 | bytes 7352320 | tf_op jit(solution)/shard_map/dot_general | solution.py:50
  93.0 0.0 all-gather.15.cloned.1.call-update
  93.0 0.0 all-gather.17.cloned.1.call-start
  93.0 0.5 all-gather.17.cloned.1.call-update
  94.3 0.0 copy-done.3
  94.3 0.1 select_reduce_fusion.1
  94.4 0.1 select_reduce_fusion
  94.5 31.4 %all-gather.11.cloned.1.call-done = bf16[2048,1024]{1,0:T(8,128)(2,1)} async-done(((bf16[256,1024]{1,0:T(8,128)(2,1)}), bf16[2048,1024]{1,0:T(8,128)(2,1)}) %all-gather.11.cloned.1.call-update) | async-done | bytes 4194320 | tf_op jit(solution)/shard_map/all_gather | solution.py:44
  126.0 4.7 %multiply_reduce_fusion = (f32[512,16]{0,1:T(8,128)S(1)}, f32[512,1024]{0,1:T(8,128)S(1)}) fusion(bf16[2048,1024]{1,0:T(8,128)(2,1)} %all-gather.11.cloned.1.call-done, bf16[512,2048]{1,0:T(8,128)(2,1)S(1)} %copy-done.1, f32[2048]{0:T(1024)S(1)} %copy-done.4, f32[512]{0:T(512)S(1)} %add_rsqrt_fusion.2, f32[512]{0:T(512)S(1)} %broadcast_multiply_fusion.1), kind=kOutput, calls=%fused_computation.37 | convolution fusion | flops 2153766912 | bytes 8433664 | tf_op jit(solution)/shard_map/dot_general | solution.py:50
  130.7 0.3 multiply_convert_fusion
  131.1 77.1 %all-gather.9.cloned.1.call-done = bf16[2048,1024]{1,0:T(8,128)(2,1)} async-done(((bf16[512,1024]{1,0:T(8,128)(2,1)}), bf16[2048,1024]{1,0:T(8,128)(2,1)}) %all-gather.9.cloned.1.call-update) | async-done | bytes 4194320 | tf_op jit(solution)/shard_map/all_gather | solution.py:82
  208.2 11.8 %reshape.112 = bf16[4,512,16,64]{3,2,1,0:T(8,128)(2,1)} reshape(bf16[2048,1024]{1,0:T(8,128)(2,1)} %all-gather.9.cloned.1.call-done) | data formatting | bytes 8388608 | tf_op jit(solution)/shard_map/reshape | solution.py:88
  220.0 9.8 %copy.29 = bf16[4,512,16,64]{1,3,2,0:T(8,128)(2,1)} copy(bf16[4,512,16,64]{3,2,1,0:T(8,128)(2,1)} %reshape.112) | data formatting | bytes 8388608
  229.8 59.2 %all-gather.15.cloned.1.call-done = bf16[2048,1024]{1,0:T(8,128)(2,1)} async-done(((bf16[512,1024]{1,0:T(8,128)(2,1)}), bf16[2048,1024]{1,0:T(8,128)(2,1)}) %all-gather.15.cloned.1.call-update) | async-done | bytes 4194320 | tf_op jit(solution)/shard_map/all_gather | solution.py:83
  288.9 11.7 %reshape.113 = bf16[4,512,16,64]{3,2,1,0:T(8,128)(2,1)} reshape(bf16[2048,1024]{1,0:T(8,128)(2,1)} %all-gather.15.cloned.1.call-done) | data formatting | bytes 8388608 | tf_op jit(solution)/shard_map/reshape | solution.py:89
  300.6 9.8 %copy.30 = bf16[4,512,16,64]{1,3,2,0:T(8,128)(2,1)} copy(bf16[4,512,16,64]{3,2,1,0:T(8,128)(2,1)} %reshape.113) | data formatting | bytes 8388608
  310.4 0.0 copy-done.2
  310.4 105.1 %while.15 = (s32[]{:T(128)}, f32[16,512]{1,0:T(8,128)S(1)}, f32[16,512]{1,0:T(8,128)S(1)}, f32[512,16,64]{0,2,1:T(8,128)}, pred[512]{0:T(512)(128)(4,1)S(1)}, /*...) while((s32[]{:T(128)}, f32[16,512]{1,0:T(8,128)S(1)}, ...), condition=%wide.region_9.10_spmd.clone, body=%wide.region_6.9_spmd.clone.sunk | while | flops 1130151936 | bytes 126356832 | solution.py:91
  310.4 0.2 broadcast_compare_fusion.2
  310.6 9.1 %fusion.58 = (f32[16,512]{1,0:T(8,128)S(1)}, f32[16,512,512]{2,1,0:T(8,128)}) fusion(f32[16]{0:T(128)S(1)} %get-tuple-element.252, pred[512,512]{0,1:T(8,128)(4,1)S(1)} %broadcast_compare_fusion.2, bf16[512,16,64]{0,2,1:T(8,128)(2,1)S(1)} %get-tuple-element.251, bf16[4,512,16,64]{1,3,2,0:T(8,128)(2,1)} %get-tuple-element.250, s32[]{:T(128)} %get-tuple-element.232), kind=kOutput, calls=%fused_computation.2.clone.1 | convolution fusion | flops 549445632 | bytes 19169856 | tf_op jit(solution)/shard_map/while/body/eval_jaxpr/ihd,jhd->hij/dot_general | solution.py:67
  319.7 0.0 copy-start
  319.7 12.5 %bitcast_add_fusion.2 = f32[512,16,64]{0,2,1:T(8,128)} fusion(f32[512,16,64]{0,2,1:T(8,128)} %get-tuple-element.235, f32[16,512,512]{2,1,0:T(8,128)} %get-tuple-element.218, f32[16,512]{1,0:T(8,128)S(1)} %get-tuple-element.245, f32[16]{0:T(128)S(1)} %get-tuple-element.252, pred[512,512]{0,1:T(8,128)(4,1)S(1)} %broadcast_compare_fusion.2, ...), kind=kOutput, calls=%fused_computation.7.clone.1 | convolution fusion | flops 559415296 | bytes 22348352 | tf_op jit(solution)/shard_map/while/body/eval_jaxpr/hij,jhd->ihd/dot_general | solution.py:75
  332.2 0.0 copy-done
  332.2 4.2 fusion.60
  336.5 0.2 broadcast_compare_fusion.2
  336.7 8.8 %fusion.58 = (f32[16,512]{1,0:T(8,128)S(1)}, f32[16,512,512]{2,1,0:T(8,128)}) fusion(f32[16]{0:T(128)S(1)} %get-tuple-element.252, pred[512,512]{0,1:T(8,128)(4,1)S(1)} %broadcast_compare_fusion.2, bf16[512,16,64]{0,2,1:T(8,128)(2,1)S(1)} %get-tuple-element.251, bf16[4,512,16,64]{1,3,2,0:T(8,128)(2,1)} %get-tuple-element.250, s32[]{:T(128)} %get-tuple-element.232), kind=kOutput, calls=%fused_computation.2.clone.1 | convolution fusion | flops 549445632 | bytes 19169856 | tf_op jit(solution)/shard_map/while/body/eval_jaxpr/ihd,jhd->hij/dot_general | solution.py:67
  345.6 12.9 %bitcast_add_fusion.2 = f32[512,16,64]{0,2,1:T(8,128)} fusion(f32[512,16,64]{0,2,1:T(8,128)} %get-tuple-element.235, f32[16,512,512]{2,1,0:T(8,128)} %get-tuple-element.218, f32[16,512]{1,0:T(8,128)S(1)} %get-tuple-element.245, f32[16]{0:T(128)S(1)} %get-tuple-element.252, pred[512,512]{0,1:T(8,128)(4,1)S(1)} %broadcast_compare_fusion.2, ...), kind=kOutput, calls=%fused_computation.7.clone.1 | convolution fusion | flops 559415296 | bytes 22348352 | tf_op jit(solution)/shard_map/while/body/eval_jaxpr/hij,jhd->ihd/dot_general | solution.py:75
  358.4 0.0 copy-done
  358.4 4.2 fusion.60
  362.7 0.2 broadcast_compare_fusion.2
  363.0 8.8 %fusion.58 = (f32[16,512]{1,0:T(8,128)S(1)}, f32[16,512,512]{2,1,0:T(8,128)}) fusion(f32[16]{0:T(128)S(1)} %get-tuple-element.252, pred[512,512]{0,1:T(8,128)(4,1)S(1)} %broadcast_compare_fusion.2, bf16[512,16,64]{0,2,1:T(8,128)(2,1)S(1)} %get-tuple-element.251, bf16[4,512,16,64]{1,3,2,0:T(8,128)(2,1)} %get-tuple-element.250, s32[]{:T(128)} %get-tuple-element.232), kind=kOutput, calls=%fused_computation.2.clone.1 | convolution fusion | flops 549445632 | bytes 19169856 | tf_op jit(solution)/shard_map/while/body/eval_jaxpr/ihd,jhd->hij/dot_general | solution.py:67
  371.8 12.9 %bitcast_add_fusion.2 = f32[512,16,64]{0,2,1:T(8,128)} fusion(f32[512,16,64]{0,2,1:T(8,128)} %get-tuple-element.235, f32[16,512,512]{2,1,0:T(8,128)} %get-tuple-element.218, f32[16,512]{1,0:T(8,128)S(1)} %get-tuple-element.245, f32[16]{0:T(128)S(1)} %get-tuple-element.252, pred[512,512]{0,1:T(8,128)(4,1)S(1)} %broadcast_compare_fusion.2, ...), kind=kOutput, calls=%fused_computation.7.clone.1 | convolution fusion | flops 559415296 | bytes 22348352 | tf_op jit(solution)/shard_map/while/body/eval_jaxpr/hij,jhd->ihd/dot_general | solution.py:75
  384.7 0.0 copy-done
  384.7 4.2 fusion.60
  389.0 0.2 broadcast_compare_fusion.2
  389.2 8.8 %fusion.58 = (f32[16,512]{1,0:T(8,128)S(1)}, f32[16,512,512]{2,1,0:T(8,128)}) fusion(f32[16]{0:T(128)S(1)} %get-tuple-element.252, pred[512,512]{0,1:T(8,128)(4,1)S(1)} %broadcast_compare_fusion.2, bf16[512,16,64]{0,2,1:T(8,128)(2,1)S(1)} %get-tuple-element.251, bf16[4,512,16,64]{1,3,2,0:T(8,128)(2,1)} %get-tuple-element.250, s32[]{:T(128)} %get-tuple-element.232), kind=kOutput, calls=%fused_computation.2.clone.1 | convolution fusion | flops 549445632 | bytes 19169856 | tf_op jit(solution)/shard_map/while/body/eval_jaxpr/ihd,jhd->hij/dot_general | solution.py:67
  398.1 12.9 %bitcast_add_fusion.2 = f32[512,16,64]{0,2,1:T(8,128)} fusion(f32[512,16,64]{0,2,1:T(8,128)} %get-tuple-element.235, f32[16,512,512]{2,1,0:T(8,128)} %get-tuple-element.218, f32[16,512]{1,0:T(8,128)S(1)} %get-tuple-element.245, f32[16]{0:T(128)S(1)} %get-tuple-element.252, pred[512,512]{0,1:T(8,128)(4,1)S(1)} %broadcast_compare_fusion.2, ...), kind=kOutput, calls=%fused_computation.7.clone.1 | convolution fusion | flops 559415296 | bytes 22348352 | tf_op jit(solution)/shard_map/while/body/eval_jaxpr/hij,jhd->ihd/dot_general | solution.py:75
  410.9 0.0 copy-done
  410.9 4.2 fusion.60
  415.4 1.9 divide_convert_fusion
  417.3 0.0 all-gather.17.cloned.1.call-done
  417.3 5.9 %fusion.24 = bf16[512,2048]{1,0:T(8,128)(2,1)} fusion(bf16[512,2048]{1,0:T(8,128)(2,1)S(1)} %copy-done.1, bf16[512,1024]{0,1:T(8,128)(2,1)S(1)} %bitcast.60, bf16[1024,2048]{1,0:T(8,128)(2,1)} %all-gather.17.cloned.1.call-done), kind=kOutput, calls=%fused_computation.33 | convolution fusion | flops 2150629376 | bytes 9437184 | tf_op jit(solution)/shard_map/dot_general | solution.py:95
  (35 shorter events, 0.4 us)
Async XLA Ops:
  6.5 4.2 copy-start.1
  6.5 42.2 %copy-start.4 = (f32[2048]{0:T(1024)S(1)}, f32[2048]{0:T(1024)}, u32[]{:S(2)}) copy-start(f32[2048]{0:T(1024)} %param.14) | copy-start | bytes 24580
  6.5 42.2 %all-gather.7.cloned.1.call-start = ((), (), s32[]{:S(2)}) async-start(), calls=%async_computation | async-start | bytes 4718592 | tf_op jit(solution)/shard_map/all_gather | solution.py:45
  7.3 80.1 %all-gather.13.cloned.1.call-start = ((), (), s32[]{:S(2)}) async-start(), calls=%async_computation.3 | async-start | bytes 4718592 | tf_op jit(solution)/shard_map/all_gather | solution.py:46
  8.0 118.0 %all-gather.11.cloned.1.call-start = ((), (), s32[]{:S(2)}) async-start(), calls=%async_computation.2 | async-start | bytes 4718592 | tf_op jit(solution)/shard_map/all_gather | solution.py:44
  8.7 199.5 %all-gather.9.cloned.1.call-start = ((), (), s32[]{:S(2)}) async-start(), calls=%async_computation.1 | async-start | bytes 5242880 | tf_op jit(solution)/shard_map/all_gather | solution.py:82
  68.3 25.9 %copy-start.3 = (s32[1,4]{1,0:T(1,128)S(1)}, s32[1,4]{1,0:T(1,128)}, u32[]{:S(2)}) copy-start(s32[1,4]{1,0:T(1,128)} %param.12) | copy-start | bytes 52
  68.4 220.6 %all-gather.15.cloned.1.call-start = ((), (), s32[]{:S(2)}) async-start(), calls=%async_computation.4 | async-start | bytes 5242880 | tf_op jit(solution)/shard_map/all_gather | solution.py:83
  93.0 324.4 %all-gather.17.cloned.1.call-start = ((), (), s32[]{:S(2)}) async-start(), calls=%async_computation.5 | async-start | bytes 4718592 | tf_op jit(solution)/shard_map/all_gather | solution.py:97
  300.6 9.8 %copy-start.2 = (f32[16]{0:T(128)S(1)}, f32[16]{0:T(128)}, u32[]{:S(2)}) copy-start(f32[16]{0:T(128)} %param.19) | copy-start | bytes 196
  319.7 12.5 %copy-start = (f32[16,512,512]{2,1,0:T(8,128)S(1)}, f32[16,512,512]{2,1,0:T(8,128)}, u32[]{:S(2)}) copy-start(f32[16,512,512]{2,1,0:T(8,128)} %get-tuple-element.218) | copy-start | bytes 50331652 | tf_op jit(solution)/shard_map/while
  345.6 12.9 %copy-start = (f32[16,512,512]{2,1,0:T(8,128)S(1)}, f32[16,512,512]{2,1,0:T(8,128)}, u32[]{:S(2)}) copy-start(f32[16,512,512]{2,1,0:T(8,128)} %get-tuple-element.218) | copy-start | bytes 50331652 | tf_op jit(solution)/shard_map/while
  371.8 12.9 %copy-start = (f32[16,512,512]{2,1,0:T(8,128)S(1)}, f32[16,512,512]{2,1,0:T(8,128)}, u32[]{:S(2)}) copy-start(f32[16,512,512]{2,1,0:T(8,128)} %get-tuple-element.218) | copy-start | bytes 50331652 | tf_op jit(solution)/shard_map/while
  398.1 12.9 %copy-start = (f32[16,512,512]{2,1,0:T(8,128)S(1)}, f32[16,512,512]{2,1,0:T(8,128)}, u32[]{:S(2)}) copy-start(f32[16,512,512]{2,1,0:T(8,128)} %get-tuple-element.218) | copy-start | bytes 50331652 | tf_op jit(solution)/shard_map/while
Sparse Core Ops, SparseCore 0:
  9.2 39.4 all-gather.6
  50.6 36.7 all-gather.12
  89.2 36.7 all-gather.10
  127.4 80.7 all-gather.8
  209.6 79.2 all-gather.14
  290.7 35.2 all-gather.16
where the time goes:
time: 432 us; the launch traced here: 430 us
  waiting for transfers between devices  227 us (53%)
  matrix products  109 us (25%)
  local copies, waits for them, and re-layouts  50.6 us (12%)
  other arithmetic  28.5 us (7%)
  between operations  14.3 us (3%)
    all_gather x1, waiting for transfers between devices, per_device(): lax.all_gather(k_flat, 'win', axis=0, tiled=True)  77.1 us
    all_gather x1, waiting for transfers between devices, per_device(): lax.all_gather(value_half, 'win', axis=0, tiled=True)  59.2 us
    dot_general x4, matrix products, attend_block(): jnp.einsum('hij,jhd->ihd', weight.astype(jnp.bfloat16), values, preferred...  51.1 us
    all_gather x1, waiting for transfers between devices, per_device(): lax.all_gather(w_key, 'fsdp', axis=0, tiled=True)  37.3 us
    dot_general x4, matrix products, attend_block(): jnp.einsum('ihd,jhd->hij', q_unit, keys, preferred_element_type=jnp.float32)  35.6 us
    all_gather x1, waiting for transfers between devices, per_device(): lax.all_gather(w_query, 'fsdp', axis=0, tiled=True)  31.4 us
    unnamed x10, local copies, waits for them, and re-layouts  19.5 us
    all_gather x1, waiting for transfers between devices, per_device(): lax.all_gather(w_value, 'fsdp', axis=0, tiled=True)  18.9 us
  transfers between devices with their start and end apart: 6, of which 5 were waited for; matrix products, arithmetic and copies ran while one was open for 42% of the time, Pallas kernels for 0%

commit v1 on v0

v1 whole, which is shorter than its diff:
```python
import functools
import math

import jax
import jax.numpy as jnp
from jax import lax
from jax.experimental import pallas as pl
from jax.experimental.pallas import tpu as pltpu
from jax.sharding import PartitionSpec as P

MESH = pl.DeviceIdType.MESH
LANES = 128
FAR = 1024.0


def layer_kernel(
    sizes,
    tokens_ref, map_ref, shift_ref, gain_ref, wq_ref, wk_ref, wv_ref, wo_ref, scale_ref,
    out_ref,
    weights, w_out, normed, sent, held, keys_t, values_1, heads_out, attended,
    load_sem, p1_send, p1_recv, p2_send, p2_recv, p3_send, p3_recv,
    a2a_send, a2a_recv, back_send, back_recv,
):
    rows_a, rows_b, groups, head_size = sizes
    tok, width = tokens_ref.shape
    cols = weights.shape[-1]
    group_heads = cols // head_size
    pairs = cols // LANES
    me = lax.axis_index("fsdp")
    mine = lax.axis_index("win")
    at_a = me // (2 * rows_b)
    at_b = (me // 2) % rows_b
    at_c = me % 2

    def index_of(a, b, c):
        return (a * rows_b + b) * 2 + c

    a_peers = [index_of((at_a + i) % rows_a, at_b, at_c) for i in range(1, rows_a)]
    b_peers = [index_of(at_a, (at_b + i) % rows_b, at_c) for i in range(1, rows_b)]
    c_peer = index_of(at_a, at_b, 1 - at_c)

    barrier = pltpu.get_barrier_semaphore()
    greeted = 0
    for peer in a_peers + b_peers + [c_peer]:
        pl.semaphore_signal(barrier, inc=1, device_id=(peer, mine), device_id_type=MESH)
        greeted += 1
    for i in range(1, groups):
        pl.semaphore_signal(
            barrier, inc=1, device_id=(me, (mine + i) % groups), device_id_type=MESH
        )
        greeted += 1

    def loads(step):
        if step == groups:
            return [pltpu.make_async_copy(wo_ref, w_out.at[at_a, at_b, at_c], load_sem.at[step, 0])]
        group = (mine + 1 + step) % groups
        window = pl.ds(pl.multiple_of(group * cols, cols), cols)
        return [
            pltpu.make_async_copy(
                source.at[:, window], weights.at[step, m, at_a, at_b, at_c], load_sem.at[step, m]
            )
            for m, source in enumerate((wq_ref, wk_ref, wv_ref))
        ]

    for step in range(groups + 1):
        for copy in loads(step):
            copy.start()
    pl.semaphore_wait(barrier, greeted)

    def view(step, a, b, c, half):
        if step == groups:
            part = w_out.shape[-1] // 2
            return w_out.at[a, b, c, :, pl.ds(half * part, part)]
        part = cols // 2
        return weights.at[step, :, a, b, c, :, pl.ds(half * part, part)]

    def everything(count):
        return pl.ds(0, count)

    def push(ref, send, recv, peer):
        return pltpu.make_async_remote_copy(
            src_ref=ref, dst_ref=ref, send_sem=send, recv_sem=recv,
            device_id=(peer, mine), device_id_type=MESH,
        )

    def phase1(step):
        for half, peers in ((0, a_peers), (1, b_peers)):
            for peer in peers:
                push(
                    view(step, at_a, at_b, at_c, half),
                    p1_send.at[step, half], p1_recv.at[step, half], peer,
                ).start()

    def phase1_size(step, half):
        if half == 0:
            return view(step, pl.ds(0, rows_a - 1), at_b, at_c, 0)
        return view(step, at_a, pl.ds(0, rows_b - 1), at_c, 1)

    def phase2(step):
        for peer in b_peers:
            push(
                view(step, everything(rows_a), at_b, at_c, 0),
                p2_send.at[step, 0], p2_recv.at[step, 0], peer,
            ).start()
        for peer in a_peers:
            push(
                view(step, at_a, everything(rows_b), at_c, 1),
                p2_send.at[step, 1], p2_recv.at[step, 1], peer,
            ).start()

    def phase2_size(step, half):
        if half == 0:
            return view(step, everything(rows_a), pl.ds(0, rows_b - 1), at_c, 0)
        return view(step, pl.ds(0, rows_a - 1), everything(rows_b), at_c, 1)

    def phase3(step):
        if step == groups:
            ref = w_out.at[:, :, at_c]
        else:
            ref = weights.at[step, :, :, :, at_c]
        return push(ref, p3_send.at[step], p3_recv.at[step], c_peer)

    def drain(ref, sem):
        pltpu.make_async_copy(ref, ref, sem).wait()

    def wait1(step):
        for half in range(2):
            drain(phase1_size(step, half), p1_recv.at[step, half])

    def wait2(step):
        for half in range(2):
            drain(phase2_size(step, half), p2_recv.at[step, half])

    def own_loaded(step):
        for copy in loads(step):
            copy.wait()

    own_loaded(0)
    phase1(0)
    own_loaded(1)

    norm_tile = min(tok, 64)

    @pl.loop(0, tok // norm_tile)
    def _(i):
        part = pl.ds(pl.multiple_of(i * norm_tile, norm_tile), norm_tile)
        resid = tokens_ref[part, :].astype(jnp.float32)
        center = jnp.mean(resid, axis=-1, keepdims=True)
        centred = resid - center
        spread = jnp.mean(centred * centred, axis=-1, keepdims=True)
        normed[part, :] = (centred * lax.rsqrt(spread + 1e-05) * gain_ref[...]).astype(jnp.bfloat16)

    tile = min(tok, 256)
    row_head = lax.broadcasted_iota(jnp.int32, (cols, cols), 0) // head_size
    col_head = lax.broadcasted_iota(jnp.int32, (cols, cols), 1) // head_size
    same_head = (row_head == col_head).astype(jnp.float32).astype(jnp.bfloat16)

    def unit(x):
        square = x * x
        high = square.astype(jnp.bfloat16)
        low = (square - high.astype(jnp.float32)).astype(jnp.bfloat16)
        total = jnp.dot(high, same_head, preferred_element_type=jnp.float32)
        total += jnp.dot(low, same_head, preferred_element_type=jnp.float32)
        return (x * lax.rsqrt(total + 1e-06)).astype(jnp.bfloat16)

    def exchange(step):
        group = (mine + 1 + step) % groups
        return pltpu.make_async_remote_copy(
            src_ref=sent.at[step], dst_ref=held.at[mine],
            send_sem=a2a_send.at[step], recv_sem=a2a_recv.at[mine],
            device_id=(me, group), device_id_type=MESH,
        )

    def project(step):
        target = held.at[mine] if step == groups - 1 else sent.at[step]

        @pl.loop(0, tok // tile)
        def _(i):
            part = pl.ds(pl.multiple_of(i * tile, tile), tile)
            x = normed[part, :]
            for m in range(3):
                w = weights[step, m].reshape(width, cols)
                y = jnp.dot(x, w, preferred_element_type=jnp.float32)
                target[m, part, :] = unit(y) if m < 2 else y.astype(jnp.bfloat16)

        if step < groups - 1:
            exchange(step).start()

    for step in range(groups + 2):
        if step <= groups:
            wait1(step)
            phase2(step)
            if step + 1 <= groups:
                if step + 1 >= 2:
                    own_loaded(step + 1)
                phase1(step + 1)
        if 1 <= step <= groups:
            phase3(step - 1).wait_recv()
            project(step - 1)
        if step <= groups:
            wait2(step)
            phase3(step).start()

    def block_region(block, shape, axis, start):
        first = map_ref[0, block] * tok + start
        return (first + lax.broadcasted_iota(jnp.int32, shape, axis) >= shift_ref[0]).astype(jnp.float32)

    def prepare(block):
        where = pl.ds(pl.multiple_of(block * tok, tok), tok)
        region = block_region(block, (LANES, tok), 1, 0)
        row = lax.broadcasted_iota(jnp.int32, (LANES, tok), 0)
        feature = jnp.where(row == 0, region - 1.0, jnp.where(row == 1, -region, 0.0)) * FAR
        feature = feature.astype(jnp.bfloat16)
        for pair in range(pairs):
            lanes = pl.ds(pair * LANES, LANES)
            keys_t[pair, 0:LANES, where] = held[block, 1, :, lanes].T
            keys_t[pair, LANES : 2 * LANES, where] = feature
            values_1[pair, where, 0:LANES] = held[block, 2, :, lanes]
            values_1[pair, where, LANES : 2 * LANES] = jnp.ones((tok, LANES), jnp.bfloat16)

    prepare(mine)
    for i in range(1, groups):
        source = (mine - i + groups) % groups
        drain(held.at[source], a2a_recv.at[source])
        prepare(source)

    lane = lax.broadcasted_iota(jnp.int32, (1, LANES), 1)
    pick = [
        (lane // head_size == hh).astype(jnp.float32).astype(jnp.bfloat16)
        for hh in range(LANES // head_size)
    ]

    def attend(block, store):
        @pl.loop(0, tok // tile)
        def _(i):
            start = pl.multiple_of(i * tile, tile)
            part = pl.ds(start, tile)
            region = block_region(block, (tile, LANES), 0, start)
            place = lax.broadcasted_iota(jnp.int32, (tile, LANES), 1)
            feature = jnp.where(place == 0, region, jnp.where(place == 1, 1.0 - region, 0.0))
            feature = feature.astype(jnp.bfloat16)
            for pair in range(pairs):
                query = held[block, 0, part, pair * LANES : (pair + 1) * LANES]
                result = None
                for hh, chosen in enumerate(pick):
                    factor = scale_ref[mine * group_heads + pair * len(pick) + hh] * math.log2(math.e)
                    q = jnp.concatenate([query * chosen, feature], axis=1)
                    score = jnp.dot(q, keys_t[pair], preferred_element_type=jnp.float32)
                    best = jnp.max(score, axis=1, keepdims=True)
                    weight = jnp.exp2((score - best) * factor).astype(jnp.bfloat16)
                    both = jnp.dot(weight, values_1[pair], preferred_element_type=jnp.float32)
                    o = both[:, 0:LANES] / both[:, LANES : 2 * LANES]
                    result = o if result is None else jnp.where(place // head_size == hh, o, result)
                store(part, pair, result.astype(jnp.bfloat16))

    def give_back(step):
        block = (mine + 1 + step) % groups
        return pltpu.make_async_remote_copy(
            src_ref=heads_out.at[step],
            dst_ref=attended.at[mine],
            send_sem=back_send.at[step], recv_sem=back_recv.at[mine],
            device_id=(me, block), device_id_type=MESH,
        )

    @pl.loop(0, groups - 1)
    def _(step):
        def store(part, pair, value):
            heads_out[step, part, pair * LANES : (pair + 1) * LANES] = value

        attend((mine + 1 + step) % groups, store)
        give_back(step).start()

    def store_own(part, pair, value):
        attended[mine, part, pair * LANES : (pair + 1) * LANES] = value

    attend(mine, store_own)
    phase3(groups).wait_recv()
    for i in range(1, groups):
        source = (mine - i + groups) % groups
        drain(attended.at[source], back_recv.at[source])

    out_tile = min(width, 512)
    inner = groups * cols

    @pl.loop(0, width // out_tile)
    def _(i):
        window = pl.ds(pl.multiple_of(i * out_tile, out_tile), out_tile)
        w = w_out[:, :, :, :, window].reshape(inner, out_tile)
        x = jnp.concatenate([attended[g] for g in range(groups)], axis=1)
        y = jnp.dot(x, w, preferred_element_type=jnp.float32)
        out_ref[:, window] = (tokens_ref[:, window].astype(jnp.float32) + y).astype(jnp.bfloat16)

    for step in range(groups + 1):
        for half in range(2):
            drain(phase1_size(step, half), p1_send.at[step, half])
            drain(phase2_size(step, half), p2_send.at[step, half])
        phase3(step).wait_send()
    for step in range(groups - 1):
        exchange(step).wait_send()
        give_back(step).wait_send()


def per_device(tokens, block_map, shift, ln_gain, w_query, w_key, w_value, w_out, logit_scale):
    tok, width = tokens.shape
    heads = logit_scale.shape[0]
    inner = w_query.shape[1]
    head_size = inner // heads
    members = lax.axis_size("fsdp")
    groups = lax.axis_size("win")
    chips = members // 2
    rows_b = 2 ** ((chips.bit_length() - 1) // 2)
    rows_a = chips // rows_b
    cols = inner // groups
    rows = w_query.shape[0]
    out_rows = w_out.shape[0]
    vmem = pl.BlockSpec(memory_space=pltpu.VMEM)
    smem = pl.BlockSpec(memory_space=pltpu.SMEM)
    far = pl.BlockSpec(memory_space=pl.ANY)
    dma = pltpu.SemaphoreType.DMA
    bf16 = jnp.bfloat16
    return pl.pallas_call(
        functools.partial(layer_kernel, (rows_a, rows_b, groups, head_size)),
        out_shape=jax.ShapeDtypeStruct((tok, width), bf16),
        in_specs=[vmem, smem, smem, vmem, far, far, far, far, smem],
        out_specs=vmem,
        scratch_shapes=[
            pltpu.VMEM((groups, 3, rows_a, rows_b, 2, rows, cols), bf16),
            pltpu.VMEM((rows_a, rows_b, 2, out_rows, width), bf16),
            pltpu.VMEM((tok, width), bf16),
            pltpu.VMEM((groups - 1, 3, tok, cols), bf16),
            pltpu.VMEM((groups, 3, tok, cols), bf16),
            pltpu.VMEM((cols // LANES, 2 * LANES, groups * tok), bf16),
            pltpu.VMEM((cols // LANES, groups * tok, 2 * LANES), bf16),
            pltpu.VMEM((groups - 1, tok, cols), bf16),
            pltpu.VMEM((groups, tok, cols), bf16),
            dma((groups + 1, 3)),
            dma((groups + 1, 2)),
            dma((groups + 1, 2)),
            dma((groups + 1, 2)),
            dma((groups + 1, 2)),
            dma((groups + 1,)),
            dma((groups + 1,)),
            dma((groups,)),
            dma((groups,)),
            dma((groups,)),
            dma((groups,)),
        ],
        compiler_params=pltpu.CompilerParams(
            collective_id=0, has_side_effects=True, vmem_limit_bytes=60 * 1024 * 1024
        ),
    )(tokens, block_map, shift, ln_gain.reshape(1, width), w_query, w_key, w_value, w_out, logit_scale)


def solution(mesh):
    return jax.shard_map(
        per_device,
        mesh=mesh,
        in_specs=(
            P(("fsdp", "win"), None),
            P("fsdp", None),
            P("fsdp"),
            P(),
            P("fsdp", None),
            P("fsdp", None),
            P("fsdp", None),
            P("fsdp", None),
            P(),
        ),
        out_specs=P(("fsdp", "win"), None),
        check_vma=False,
    )
```

time: 432 us -> 136 us (0.31)
  waiting for transfers between devices: 227 us -> 0 us
  Pallas kernels: 0 us -> 132 us
  matrix products: 109 us -> 0 us
  local copies, waits for them, and re-layouts: 50.6 us -> 3.16 us
  other arithmetic: 28.5 us -> 0 us
  between operations: 14.3 us -> 0.66 us
    all_gather x6 -> x0, waiting for transfers between devices: 224 us -> none  [the longest x1 77.1 us: per_device(): lax.all_gather(k_flat, 'win', axis=0, tiled=True)]
    pallas_call x0 -> x1, Pallas kernels: none -> 132 us  [per_device(): pl.pallas_call(functools.partial(layer_kernel, (rows_a, rows_b, groups, h...]
    dot_general x12 -> x0, matrix products: 109 us -> none  [the longest x4 51.1 us: attend_block(): jnp.einsum('hij,jhd->ihd', weight.astype(jnp.bfloat16), values, preferred...]
    reshape x2 -> x0, local copies, waits for them, and re-layouts: 23.5 us -> none  [the longest x1 11.8 us: per_device(): keys = pieces[0].reshape(nblk, blk, head_count, head_size)]
    reduce_sum x9 -> x0, other arithmetic: 21.7 us -> none  [the longest x4 16.8 us: attend_block(): total = total * fade + jnp.sum(weight, axis=-1)]
    unnamed x10 -> x1, local copies, waits for them, and re-layouts: 19.5 us -> 3.16 us
    mul x4 -> x0, local copies, waits for them, and re-layouts: 7.46 us -> none  [the longest x2 4.52 us: unit_heads(): return (split * scale).astype(jnp.bfloat16)]
    convert_element_type x3 -> x0, other arithmetic: 5.7 us -> none  [the longest x2 3.82 us: unit_heads(): return (split * scale).astype(jnp.bfloat16)]
  transfers between devices with their start and end apart: 6 -> 0, of which waited for: 5 -> 0; matrix products, arithmetic and copies ran while one was open for 42% -> 0% of each run, Pallas kernels for 0% -> 0%
where the time goes in v1:
time: 136 us
  Pallas kernels  132 us (97%)
  local copies, waits for them, and re-layouts  3.16 us (2%)
    pallas_call x1, Pallas kernels, per_device(): pl.pallas_call(functools.partial(layer_kernel, (rows_a, rows_b, groups, h...  132 us
    unnamed x1, local copies, waits for them, and re-layouts  3.16 us

profile of v1, /device:TPU:0, one launch (start us, length us, event | category | flops | bytes accessed | tf_op | source)
XLA Modules:
  0.0 136.3 jit_solution(3103921410542244403)
XLA Ops:
  0.7 132.5 %shard_map.91 = bf16[512,2048]{1,0:T(8,128)(2,1)} custom-call(bf16[512,2048]{1,0:T(8,128)(2,1)} %tokens_ref.1, s32[1,4]{1,0:T(1,128)} %map_ref.1, s32[1]{0:T(128)S(6)} %copy.11.shift_ref, f32[1,2048]{1,0:T(1,128)} %bitcast.1, bf16[256,1024]{1,0:T(8,128)(2,1)} %wq_ref.1, bf16[256,1024]{1,0:T(8,128)(2,1)} %wk_ref.1, bf16[256,1024]{1,0:T(8,128)(2,1)} %wv_ref.1, ...), custom_call_target="tpu_custom_call" | custom-call | tf_op jit(solution)/shard_map/pallas_call | solution.py:321
  133.1 3.2 %copy.12 = bf16[512,2048]{1,0:T(8,128)(2,1)} copy(bf16[512,2048]{1,0:T(8,128)(2,1)} %shard_map.91) | data formatting | bytes 4194304

commit v2 on v1

v2 whole, which is shorter than its diff:
```python
import functools
import math

import jax
import jax.numpy as jnp
from jax import lax
from jax.experimental import pallas as pl
from jax.experimental.pallas import tpu as pltpu
from jax.sharding import PartitionSpec as P

MESH = pl.DeviceIdType.MESH
LANES = 128
FAR = 1024.0


def layer_kernel(
    sizes,
    tokens_ref, map_ref, shift_ref, gain_ref, wq_ref, wk_ref, wv_ref, wo_ref, scale_ref,
    out_ref,
    weights, w_out, normed, sent, held, keys_t, values_1, heads_out, attended,
    load_sem, p1_send, p1_recv, p2_send, p2_recv, p3_send, p3_recv,
    a2a_send, a2a_recv, back_send, back_recv,
):
    rows_a, rows_b, groups, head_size, pairs = sizes
    tok, width = tokens_ref.shape
    rows = wq_ref.shape[0]
    cols = pairs * LANES
    group_heads = cols // head_size
    last = groups * pairs
    me = lax.axis_index("fsdp")
    mine = lax.axis_index("win")
    at_a = me // (2 * rows_b)
    at_b = (me // 2) % rows_b
    at_c = me % 2

    def index_of(a, b, c):
        return (a * rows_b + b) * 2 + c

    a_peers = [index_of((at_a + i) % rows_a, at_b, at_c) for i in range(1, rows_a)]
    b_peers = [index_of(at_a, (at_b + i) % rows_b, at_c) for i in range(1, rows_b)]
    c_peer = index_of(at_a, at_b, 1 - at_c)

    barrier = pltpu.get_barrier_semaphore()
    greeted = 0
    for peer in a_peers + b_peers + [c_peer]:
        pl.semaphore_signal(barrier, inc=1, device_id=(peer, mine), device_id_type=MESH)
        greeted += 1
    for i in range(1, groups):
        pl.semaphore_signal(
            barrier, inc=1, device_id=(me, (mine + i) % groups), device_id_type=MESH
        )
        greeted += 1

    offsets = [(i + groups // 2 - 1) % groups + 1 for i in range(groups)]
    offsets = [i for i in offsets if i != groups] + [0]

    def group_of(step):
        return (mine + offsets[step % groups]) % groups

    def loads(step):
        if step == last:
            return [pltpu.make_async_copy(wo_ref, w_out.at[at_a, at_b, at_c], load_sem.at[step, 0])]
        first = group_of(step) * cols + (step // groups) * LANES
        window = pl.ds(pl.multiple_of(first, LANES), LANES)
        return [
            pltpu.make_async_copy(
                source.at[:, window],
                weights.at[step, at_a, at_b, at_c, :, pl.ds(m * LANES, LANES)],
                load_sem.at[step, m],
            )
            for m, source in enumerate((wq_ref, wk_ref, wv_ref))
        ]

    for step in range(last + 1):
        for copy in loads(step):
            copy.start()
    pl.semaphore_wait(barrier, greeted)

    def view(step, a, b, c, half):
        if step == last:
            part = w_out.shape[-1] // 2
            return w_out.at[a, b, c, :, pl.ds(half * part, part)]
        part = rows // 2
        return weights.at[step, a, b, c, pl.ds(half * part, part), :]

    def everything(count):
        return pl.ds(0, count)

    def push(ref, send, recv, peer):
        return pltpu.make_async_remote_copy(
            src_ref=ref, dst_ref=ref, send_sem=send, recv_sem=recv,
            device_id=(peer, mine), device_id_type=MESH,
        )

    def phase1(step):
        for half, peers in ((0, a_peers), (1, b_peers)):
            for peer in peers:
                push(
                    view(step, at_a, at_b, at_c, half),
                    p1_send.at[step, half], p1_recv.at[step, half], peer,
                ).start()

    def phase1_size(step, half):
        if half == 0:
            return view(step, pl.ds(0, rows_a - 1), at_b, at_c, 0)
        return view(step, at_a, pl.ds(0, rows_b - 1), at_c, 1)

    def phase2(step):
        for peer in b_peers:
            push(
                view(step, everything(rows_a), at_b, at_c, 0),
                p2_send.at[step, 0], p2_recv.at[step, 0], peer,
            ).start()
        for peer in a_peers:
            push(
                view(step, at_a, everything(rows_b), at_c, 1),
                p2_send.at[step, 1], p2_recv.at[step, 1], peer,
            ).start()

    def phase2_size(step, half):
        if half == 0:
            return view(step, everything(rows_a), pl.ds(0, rows_b - 1), at_c, 0)
        return view(step, pl.ds(0, rows_a - 1), everything(rows_b), at_c, 1)

    def phase3(step):
        ref = w_out.at[:, :, at_c] if step == last else weights.at[step, :, :, at_c]
        return push(ref, p3_send.at[step], p3_recv.at[step], c_peer)

    def drain(ref, sem):
        pltpu.make_async_copy(ref, ref, sem).wait()

    def wait1(step):
        for half in range(2):
            drain(phase1_size(step, half), p1_recv.at[step, half])

    def wait2(step):
        for half in range(2):
            drain(phase2_size(step, half), p2_recv.at[step, half])

    def own_loaded(step):
        for copy in loads(step):
            copy.wait()

    norm_tile = min(tok // 2, 64)

    def normalize(half):
        @pl.loop(0, tok // 2 // norm_tile)
        def _(i):
            start = half * (tok // 2) + i * norm_tile
            part = pl.ds(pl.multiple_of(start, norm_tile), norm_tile)
            resid = tokens_ref[part, :].astype(jnp.float32)
            center = jnp.mean(resid, axis=-1, keepdims=True)
            centred = resid - center
            spread = jnp.mean(centred * centred, axis=-1, keepdims=True)
            value = centred * lax.rsqrt(spread + 1e-05) * gain_ref[...]
            normed[part, :] = value.astype(jnp.bfloat16)

    own_loaded(0)
    phase1(0)
    normalize(0)

    tile = min(tok, 256)
    row_head = lax.broadcasted_iota(jnp.int32, (LANES, LANES), 0) // head_size
    col_head = lax.broadcasted_iota(jnp.int32, (LANES, LANES), 1) // head_size
    same_head = (row_head == col_head).astype(jnp.float32).astype(jnp.bfloat16)

    def unit(x):
        square = x * x
        high = square.astype(jnp.bfloat16)
        low = (square - high.astype(jnp.float32)).astype(jnp.bfloat16)
        total = jnp.dot(high, same_head, preferred_element_type=jnp.float32)
        total += jnp.dot(low, same_head, preferred_element_type=jnp.float32)
        return (x * lax.rsqrt(total + 1e-06)).astype(jnp.bfloat16)

    def slot(step):
        return (step // groups) * (groups - 1) + step % groups

    def exchange(step):
        pair = step // groups
        return pltpu.make_async_remote_copy(
            src_ref=sent.at[slot(step)], dst_ref=held.at[pair, mine],
            send_sem=a2a_send.at[slot(step)], recv_sem=a2a_recv.at[pair, mine],
            device_id=(me, group_of(step)), device_id_type=MESH,
        )

    remote_steps = [step for step in range(last) if step % groups < groups - 1]

    def project(step):
        remote = step in remote_steps
        target = sent.at[slot(step)] if remote else held.at[step // groups, mine]

        @pl.loop(0, tok // tile)
        def _(i):
            part = pl.ds(pl.multiple_of(i * tile, tile), tile)
            w = weights[step].reshape(width, 3 * LANES)
            y = jnp.dot(normed[part, :], w, preferred_element_type=jnp.float32)
            target[0, part, :] = unit(y[:, 0:LANES])
            target[1, part, :] = unit(y[:, LANES : 2 * LANES])
            target[2, part, :] = y[:, 2 * LANES :].astype(jnp.bfloat16)

        if remote:
            exchange(step).start()

    for step in range(last + 1):
        wait1(step)
        phase2(step)
        if step < last:
            own_loaded(step + 1)
            phase1(step + 1)
        if step == 0:
            normalize(1)
        else:
            wait2(step - 1)
            phase3(step - 1).start()
            phase3(step - 1).wait_recv()
            project(step - 1)

    def block_region(block, shape, axis, start):
        first = map_ref[0, block] * tok + start
        return (first + lax.broadcasted_iota(jnp.int32, shape, axis) >= shift_ref[0]).astype(jnp.float32)

    def prepare(pair, block):
        where = pl.ds(pl.multiple_of(block * tok, tok), tok)
        region = block_region(block, (LANES, tok), 1, 0)
        row = lax.broadcasted_iota(jnp.int32, (LANES, tok), 0)
        feature = jnp.where(row == 0, region - 1.0, jnp.where(row == 1, -region, 0.0)) * FAR
        keys_t[pair, 0:LANES, where] = held[pair, block, 1].T
        keys_t[pair, LANES : 2 * LANES, where] = feature.astype(jnp.bfloat16)
        values_1[pair, where, 0:LANES] = held[pair, block, 2]
        values_1[pair, where, LANES : 2 * LANES] = jnp.ones((tok, LANES), jnp.bfloat16)

    def prepare_all(pair):
        prepare(pair, mine)
        for offset in offsets[:-1]:
            source = (mine - offset + groups) % groups
            drain(held.at[pair, source], a2a_recv.at[pair, source])
            prepare(pair, source)

    lane = lax.broadcasted_iota(jnp.int32, (1, LANES), 1)
    pick = [
        (lane // head_size == hh).astype(jnp.float32).astype(jnp.bfloat16)
        for hh in range(LANES // head_size)
    ]

    def attend(pair, block, target):
        @pl.loop(0, tok // tile)
        def _(i):
            start = pl.multiple_of(i * tile, tile)
            part = pl.ds(start, tile)
            region = block_region(block, (tile, LANES), 0, start)
            place = lax.broadcasted_iota(jnp.int32, (tile, LANES), 1)
            feature = jnp.where(place == 0, region, jnp.where(place == 1, 1.0 - region, 0.0))
            feature = feature.astype(jnp.bfloat16)
            query = held[pair, block, 0, part, :]
            result = None
            for hh, chosen in enumerate(pick):
                factor = scale_ref[mine * group_heads + pair * len(pick) + hh] * math.log2(math.e)
                q = jnp.concatenate([query * chosen, feature], axis=1)
                score = jnp.dot(q, keys_t[pair], preferred_element_type=jnp.float32)
                best = jnp.max(score, axis=1, keepdims=True)
                weight = jnp.exp2((score - best) * factor).astype(jnp.bfloat16)
                both = jnp.dot(weight, values_1[pair], preferred_element_type=jnp.float32)
                o = both[:, 0:LANES] / both[:, LANES : 2 * LANES]
                result = o if result is None else jnp.where(place // head_size == hh, o, result)
            target[part, :] = result.astype(jnp.bfloat16)

    def give_back(step):
        pair = step // groups
        return pltpu.make_async_remote_copy(
            src_ref=heads_out.at[slot(step)], dst_ref=attended.at[mine, pair],
            send_sem=back_send.at[slot(step)], recv_sem=back_recv.at[pair, mine],
            device_id=(me, group_of(step)), device_id_type=MESH,
        )

    for step in range(last):
        pair = step // groups
        if step % groups == 0:
            prepare_all(pair)
        if step in remote_steps:
            attend(pair, group_of(step), heads_out.at[slot(step)])
            give_back(step).start()
        else:
            attend(pair, mine, attended.at[mine, pair])
        if step == 0:
            wait2(last)
            phase3(last).start()

    phase3(last).wait_recv()
    for pair in range(pairs):
        for offset in offsets[:-1]:
            source = (mine - offset + groups) % groups
            drain(attended.at[source, pair], back_recv.at[pair, source])

    out_tile = min(width, 512)
    inner = groups * cols

    @pl.loop(0, width // out_tile)
    def _(i):
        window = pl.ds(pl.multiple_of(i * out_tile, out_tile), out_tile)
        w = w_out[:, :, :, :, window].reshape(inner, out_tile)
        x = jnp.concatenate(
            [attended[g, pair] for g in range(groups) for pair in range(pairs)], axis=1
        )
        y = jnp.dot(x, w, preferred_element_type=jnp.float32)
        out_ref[:, window] = (tokens_ref[:, window].astype(jnp.float32) + y).astype(jnp.bfloat16)

    for step in range(last + 1):
        for half in range(2):
            drain(phase1_size(step, half), p1_send.at[step, half])
            drain(phase2_size(step, half), p2_send.at[step, half])
        phase3(step).wait_send()
    for step in remote_steps:
        exchange(step).wait_send()
        give_back(step).wait_send()


def per_device(tokens, block_map, shift, ln_gain, w_query, w_key, w_value, w_out, logit_scale):
    tok, width = tokens.shape
    heads = logit_scale.shape[0]
    inner = w_query.shape[1]
    head_size = inner // heads
    members = lax.axis_size("fsdp")
    groups = lax.axis_size("win")
    chips = members // 2
    rows_b = 2 ** ((chips.bit_length() - 1) // 2)
    rows_a = chips // rows_b
    pairs = inner // groups // LANES
    steps = groups * pairs
    rows = w_query.shape[0]
    out_rows = w_out.shape[0]
    vmem = pl.BlockSpec(memory_space=pltpu.VMEM)
    smem = pl.BlockSpec(memory_space=pltpu.SMEM)
    far = pl.BlockSpec(memory_space=pl.ANY)
    dma = pltpu.SemaphoreType.DMA
    bf16 = jnp.bfloat16
    return pl.pallas_call(
        functools.partial(layer_kernel, (rows_a, rows_b, groups, head_size, pairs)),
        out_shape=jax.ShapeDtypeStruct((tok, width), bf16),
        in_specs=[vmem, smem, smem, vmem, far, far, far, far, smem],
        out_specs=vmem,
        scratch_shapes=[
            pltpu.VMEM((steps, rows_a, rows_b, 2, rows, 3 * LANES), bf16),
            pltpu.VMEM((rows_a, rows_b, 2, out_rows, width), bf16),
            pltpu.VMEM((tok, width), bf16),
            pltpu.VMEM((pairs * (groups - 1), 3, tok, LANES), bf16),
            pltpu.VMEM((pairs, groups, 3, tok, LANES), bf16),
            pltpu.VMEM((pairs, 2 * LANES, groups * tok), bf16),
            pltpu.VMEM((pairs, groups * tok, 2 * LANES), bf16),
            pltpu.VMEM((pairs * (groups - 1), tok, LANES), bf16),
            pltpu.VMEM((groups, pairs, tok, LANES), bf16),
            dma((steps + 1, 3)),
            dma((steps + 1, 2)),
            dma((steps + 1, 2)),
            dma((steps + 1, 2)),
            dma((steps + 1, 2)),
            dma((steps + 1,)),
            dma((steps + 1,)),
            dma((pairs * (groups - 1),)),
            dma((pairs, groups)),
            dma((pairs * (groups - 1),)),
            dma((pairs, groups)),
        ],
        compiler_params=pltpu.CompilerParams(
            collective_id=0, has_side_effects=True, vmem_limit_bytes=60 * 1024 * 1024
        ),
    )(tokens, block_map, shift, ln_gain.reshape(1, width), w_query, w_key, w_value, w_out, logit_scale)


def solution(mesh):
    return jax.shard_map(
        per_device,
        mesh=mesh,
        in_specs=(
            P(("fsdp", "win"), None),
            P("fsdp", None),
            P("fsdp"),
            P(),
            P("fsdp", None),
            P("fsdp", None),
            P("fsdp", None),
            P("fsdp", None),
            P(),
        ),
        out_specs=P(("fsdp", "win"), None),
        check_vma=False,
    )
```

time: 136 us -> 123 us (0.904); the launches traced: 136 us -> 121 us
  Pallas kernels: 132 us -> 117 us
    pallas_call x1, Pallas kernels: 132 us -> 117 us  [per_device(): pl.pallas_call(functools.partial(layer_kernel, (rows_a, rows_b, groups, h...]
where the time goes in v2:
time: 123 us; the launch traced here: 121 us
  Pallas kernels  117 us (95%)
  local copies, waits for them, and re-layouts  3.16 us (3%)
    pallas_call x1, Pallas kernels, per_device(): pl.pallas_call(functools.partial(layer_kernel, (rows_a, rows_b, groups, h...  117 us
    unnamed x1, local copies, waits for them, and re-layouts  3.16 us

profile of v2, /device:TPU:0, one launch (start us, length us, event | category | flops | bytes accessed | tf_op | source)
XLA Modules:
  0.0 121.1 jit_solution(14578869148865357637)
XLA Ops:
  0.7 117.3 %shard_map.91 = bf16[512,2048]{1,0:T(8,128)(2,1)} custom-call(bf16[512,2048]{1,0:T(8,128)(2,1)} %tokens_ref.1, s32[1,4]{1,0:T(1,128)} %map_ref.1, s32[1]{0:T(128)S(6)} %copy.11.shift_ref, f32[1,2048]{1,0:T(1,128)} %bitcast.1, bf16[256,1024]{1,0:T(8,128)(2,1)} %wq_ref.1, bf16[256,1024]{1,0:T(8,128)(2,1)} %wk_ref.1, bf16[256,1024]{1,0:T(8,128)(2,1)} %wv_ref.1, ...), custom_call_target="tpu_custom_call" | custom-call | tf_op jit(solution)/shard_map/pallas_call | solution.py:336
  117.9 3.2 %copy.12 = bf16[512,2048]{1,0:T(8,128)(2,1)} copy(bf16[512,2048]{1,0:T(8,128)(2,1)} %shard_map.91) | data formatting | bytes 4194304

commit v3 on v2

--- a/solution.py
+++ b/solution.py
@@ -201,19 +201,21 @@
         if remote:
             exchange(step).start()
 
-    for step in range(last + 1):
+    order = remote_steps + [step for step in range(last) if step not in remote_steps] + [last]
+    for turn, step in enumerate(order):
         wait1(step)
         phase2(step)
-        if step < last:
-            own_loaded(step + 1)
-            phase1(step + 1)
-        if step == 0:
+        if turn == 0:
             normalize(1)
-        else:
-            wait2(step - 1)
-            phase3(step - 1).start()
-            phase3(step - 1).wait_recv()
-            project(step - 1)
+        if step != last:
+            own_loaded(order[turn + 1])
+            phase1(order[turn + 1])
+        if turn > 0:
+            before = order[turn - 1]
+            wait2(before)
+            phase3(before).start()
+            phase3(before).wait_recv()
+            project(before)
 
     def block_region(block, shape, axis, start):
         first = map_ref[0, block] * tok + start
@@ -234,6 +236,10 @@
         for offset in offsets[:-1]:
             source = (mine - offset + groups) % groups
             drain(held.at[pair, source], a2a_recv.at[pair, source])
+            if pair > 0 and offset == offsets[-2]:
+                for step in remote_steps:
+                    if step // groups == pair - 1:
+                        give_back(step).start()
             prepare(pair, source)
 
     lane = lax.broadcasted_iota(jnp.int32, (1, LANES), 1)
@@ -278,7 +284,8 @@
             prepare_all(pair)
         if step in remote_steps:
             attend(pair, group_of(step), heads_out.at[slot(step)])
-            give_back(step).start()
+            if pair == pairs - 1:
+                give_back(step).start()
         else:
             attend(pair, mine, attended.at[mine, pair])
         if step == 0:

time: 123 us -> 122 us (level)
  no operation moved by 1% of the time
where the time goes in v3:
time: 122 us; the launch traced here: 120 us
  Pallas kernels  116 us (95%)
  local copies, waits for them, and re-layouts  3.16 us (3%)
    pallas_call x1, Pallas kernels, per_device(): pl.pallas_call(functools.partial(layer_kernel, (rows_a, rows_b, groups, h...  116 us
    unnamed x1, local copies, waits for them, and re-layouts  3.16 us

profile of v3, /device:TPU:0, one launch (start us, length us, event | category | flops | bytes accessed | tf_op | source)
XLA Modules:
  0.0 119.9 jit_solution(10155254004036311897)
XLA Ops:
  0.7 116.1 %shard_map.91 = bf16[512,2048]{1,0:T(8,128)(2,1)} custom-call(bf16[512,2048]{1,0:T(8,128)(2,1)} %tokens_ref.1, s32[1,4]{1,0:T(1,128)} %map_ref.1, s32[1]{0:T(128)S(6)} %copy.11.shift_ref, f32[1,2048]{1,0:T(1,128)} %bitcast.1, bf16[256,1024]{1,0:T(8,128)(2,1)} %wq_ref.1, bf16[256,1024]{1,0:T(8,128)(2,1)} %wk_ref.1, bf16[256,1024]{1,0:T(8,128)(2,1)} %wv_ref.1, ...), custom_call_target="tpu_custom_call" | custom-call | tf_op jit(solution)/shard_map/pallas_call | solution.py:343
  116.7 3.2 %copy.12 = bf16[512,2048]{1,0:T(8,128)(2,1)} copy(bf16[512,2048]{1,0:T(8,128)(2,1)} %shard_map.91) | data formatting | bytes 4194304
